TPU v7x, 32 devices: a whole 2x2x4 slice. The times are simulated.
32 devices in a mesh: groups: 2 (over y), rows: 4 (over x, core), seq: 4 (over z).
Axes of the slice: x: 2, y: 2, z: 4, core: 2. Of those that a mesh axis runs over, the one named last changes fastest.
Arguments:
- activations: bfloat16 [2, 8, 512, 4096], P(None, ('groups', 'rows'), 'seq'), parts along dimension 1, may hold values from -6 to 6
- out_grads: bfloat16 [2, 8, 512, 4096], P(None, ('groups', 'rows'), 'seq'), parts along dimension 1, may hold values from -6 to 6
- lengths: int32 [8], P(('groups', 'rows')), parts along dimension 0, may hold values from 64 to 512
- proj_in: bfloat16 [2, 4096, 64], replicated, may hold values from -0.09375 to 0.09375
- proj_out: bfloat16 [2, 4096, 64], replicated, may hold values from -0.09375 to 0.09375
- basis_in: float32 [2, 64, 64], replicated, may hold values from -0.75 to 0.75
- basis_out: float32 [2, 64, 64], replicated, may hold values from -0.75 to 0.75
- eigen: float32 [2, 64, 64], replicated, may hold values from 10 to 1000
- store: bfloat16 [1024, 8192], P(('groups', 'rows', 'seq')), parts along dimension 0, may hold values from -0.0625 to 0.0625
- candidates: int32 [8, 64], P('groups'), parts along dimension 0, may hold values from 0 to 511
Outputs:
- scores: float32 [1024, 4], P(('groups', 'rows', 'seq')), parts along dimension 0
- picked: float32 [8, 64], P('groups'), parts along dimension 0
There are 2 independent parts, one for each index of `groups`. A program takes and returns all parts, laid end to end along the dimension named above; an argument that names none is the same for every part. Nothing has to cross between parts.
All inputs are finite; a program needn't handle non-finite values.
Results may differ from a plain program's by a relative error of at most 0.005.
Values may be sent and summed in bfloat16 or wider, within the bound.
A program may use at most 64 MiB of HBM per device.

v0:
```python
import jax
import jax.numpy as jnp
from jax import lax
from jax.sharding import PartitionSpec as P

damping = 1.0


def body(
    activations,
    out_grads,
    lengths,
    proj_in,
    proj_out,
    basis_in,
    basis_out,
    eigen,
    store,
    candidates,
):
    nl, bdev, tok, width = activations.shape
    high = lax.Precision.HIGHEST
    offset = lax.axis_index("seq") * tok
    positions = offset + jnp.arange(tok, dtype=jnp.int32)
    mask = (positions[None, :] < lengths[:, None]).astype(jnp.bfloat16)
    pa = jnp.einsum("lbtd,ldr->lbtr", activations, proj_in, preferred_element_type=jnp.float32)
    pg = jnp.einsum("lbtd,ldr->lbtr", out_grads, proj_out, preferred_element_type=jnp.float32)
    pa = pa.astype(jnp.bfloat16) * mask[None, :, :, None]
    pg = pg.astype(jnp.bfloat16) * mask[None, :, :, None]
    local = jnp.einsum("lbto,lbti->lboi", pg, pa, preferred_element_type=jnp.float32)
    total = lax.psum(local, "seq")
    rot = jnp.einsum("loj,lboi,lik->lbjk", basis_out, total, basis_in, precision=high)
    pre = rot / (eigen[:, None] + damping)
    back = jnp.einsum("loj,lbjk,lik->lboi", basis_out, pre, basis_in, precision=high)
    test = jnp.transpose(back, (1, 0, 2, 3)).reshape(bdev, -1).astype(jnp.bfloat16)
    scores = jnp.dot(
        store,
        lax.all_gather(test, "rows", axis=0, tiled=True).T,
        preferred_element_type=jnp.float32,
    )
    rdev = store.shape[0]
    row_start = (lax.axis_index("rows") * lax.axis_size("seq") + lax.axis_index("seq")) * rdev
    local_index = candidates - row_start
    onehot = (local_index[:, :, None] == jnp.arange(rdev, dtype=jnp.int32)[None, None, :]).astype(
        jnp.float32
    )
    picked_local = jnp.einsum("bkr,rb->bk", onehot, scores, precision=high)
    picked = lax.psum(picked_local, ("rows", "seq"))
    return (scores, picked)


def solution(mesh):
    placed = (
        P(None, ("groups", "rows"), "seq", None),
        P(None, ("groups", "rows"), "seq", None),
        P(("groups", "rows")),
        P(),
        P(),
        P(),
        P(),
        P(),
        P(("groups", "rows", "seq"), None),
        P("groups", None),
    )
    return jax.shard_map(
        body,
        mesh=mesh,
        in_specs=placed,
        out_specs=(P(("groups", "rows", "seq"), None), P("groups", None)),
        check_vma=False,
    )
```

profile of v0, /device:TPU:0, one launch (start us, length us, event | category | flops | bytes accessed | tf_op | source)
XLA Modules:
  0.0 67.5 jit_solution(14491491141330753)
XLA Ops:
  0.6 0.0 copy-start
  0.6 0.0 copy-start.1
  1.5 0.8 %copy-done = bf16[2,1,128,4096]{3,2,1,0:T(8,128)(2,1)S(1)} copy-done((bf16[2,1,128,4096]{3,2,1,0:T(8,128)(2,1)S(1)}, bf16[2,1,128,4096]{3,2,1,0:T(8,128)(2,1)}, u32[]{:S(2)}) %copy-start) | copy-done | bytes 2097176
  2.2 2.1 %fusion.16 = bf16[2,128,64]{1,2,0:T(8,128)(2,1)S(1)} fusion(bf16[2,4096,64]{1,2,0:T(8,128)(2,1)} %param.14, bf16[2,1,128,4096]{3,2,1,0:T(8,128)(2,1)S(1)} %copy-done, bf16[128]{0:T(256)(128)(2,1)S(1)} %compare_convert_fusion), kind=kOutput, calls=%fused_computation.10 | convolution fusion | flops 134250496 | bytes 3178752 | tf_op jit(solution)/shard_map/lbtd,ldr->lbtr/dot_general | solution.py:27
  4.3 0.0 copy-done.1
  4.3 0.0 copy-start.2
  4.3 0.0 copy-start.3
  4.3 0.0 copy-start.4
  4.4 0.0 copy-start.5
  4.4 2.7 %fusion.14 = f32[2,64,64]{2,1,0:T(8,128)S(1)} fusion(bf16[2,128,64]{1,2,0:T(8,128)(2,1)S(1)} %fusion.16, bf16[2,4096,64]{1,2,0:T(8,128)(2,1)S(1)} %copy-done.1, bf16[2,1,128,4096]{3,2,1,0:T(8,128)(2,1)} %param.10, bf16[128]{0:T(256)(128)(2,1)S(1)} %compare_convert_fusion), kind=kOutput, calls=%fused_computation.9 | convolution fusion | flops 136347648 | bytes 3211520 | tf_op jit(solution)/shard_map/lbto,lbti->lboi/dot_general | solution.py:30
  7.0 21.5 %psum.14 = f32[2,64,64]{2,1,0:T(8,128)S(1)} all-reduce(f32[2,64,64]{2,1,0:T(8,128)S(1)} %fusion.14), channel_id=1, replica_groups=mesh['groups'=2,'rows'=4,'seq'=4] {'seq'}, use_global_device_ids=true, to_apply=%region_0.0 | all-reduce | flops 8192 | bytes 65536 | tf_op jit(solution)/shard_map/psum | solution.py:31
  28.6 0.0 copy-done.2
  28.6 0.3 fusion.25
  28.9 0.0 copy-done.3
  28.9 0.0 copy-done.4
  28.9 0.2 convolution_divide_fusion
  29.1 0.2 fusion.26
  29.3 0.2 convolution_convert_fusion
  29.5 0.1 reshape.69
  29.6 5.4 %all-gather = bf16[4,1,8192]{2,1,0:T(2,128)(2,1)S(1)} all-gather(bf16[1,1,8192]{2,1,0:T(2,128)(2,1)S(1)} %reshape.69), channel_id=1, replica_groups=mesh['groups'=2,'rows'=4,'seq'=4] {'rows'}, dimensions={0}, use_global_device_ids=true | all-gather | bytes 81920 | tf_op jit(solution)/shard_map/all_gather | solution.py:38
  35.0 1.3 %fusion.20 = f32[4,32]{1,0:T(4,128)S(1)} fusion(bf16[32,8192]{1,0:T(8,128)(2,1)} %param.18, bf16[4,1,8192]{2,1,0:T(2,128)(2,1)S(1)} %all-gather), kind=kOutput, calls=%fused_computation.13 | convolution fusion | flops 2097152 | bytes 590336 | tf_op jit(solution)/shard_map/dot_general | solution.py:36
  36.3 0.3 fusion.19
  36.6 30.9 %psum.15 = f32[4,64]{1,0:T(4,128)} all-reduce(f32[4,64]{1,0:T(4,128)S(1)} %bitcast.41), channel_id=1, replica_groups=mesh['groups'=2,'rows'=4,'seq'=4] {'rows','seq'}, use_global_device_ids=true, to_apply=%region_1.0 | all-reduce | flops 256 | bytes 2048 | tf_op jit(solution)/shard_map/psum | solution.py:48
  67.5 0.0 copy-done.6
  (4 shorter events, 0.0 us)
Async XLA Ops:
  0.6 1.6 %copy-start = (bf16[2,1,128,4096]{3,2,1,0:T(8,128)(2,1)S(1)}, bf16[2,1,128,4096]{3,2,1,0:T(8,128)(2,1)}, u32[]{:S(2)}) copy-start(bf16[2,1,128,4096]{3,2,1,0:T(8,128)(2,1)} %param.11) | copy-start | bytes 6291460
  0.6 3.7 %copy-start.1 = (bf16[2,4096,64]{1,2,0:T(8,128)(2,1)S(1)}, bf16[2,4096,64]{1,2,0:T(8,128)(2,1)}, u32[]{:S(2)}) copy-start(bf16[2,4096,64]{1,2,0:T(8,128)(2,1)} %param.13) | copy-start | bytes 3145732
  4.3 24.2 %copy-start.2 = (f32[2,64,64]{2,1,0:T(8,128)S(1)}, f32[2,64,64]{2,1,0:T(8,128)}, u32[]{:S(2)}) copy-start(f32[2,64,64]{2,1,0:T(8,128)} %param.16) | copy-start | bytes 98308
  4.3 24.5 %copy-start.3 = (f32[2,64,64]{2,1,0:T(8,128)S(1)}, f32[2,64,64]{2,1,0:T(8,128)}, u32[]{:S(2)}) copy-start(f32[2,64,64]{2,1,0:T(8,128)} %param.15) | copy-start | bytes 98308
  4.3 24.5 %copy-start.4 = (f32[2,64,64]{2,1,0:T(8,128)S(1)}, f32[2,64,64]{2,1,0:T(8,128)}, u32[]{:S(2)}) copy-start(f32[2,64,64]{2,1,0:T(8,128)} %param.17) | copy-start | bytes 98308
  4.4 32.0 %copy-start.5 = (s32[4,64]{1,0:T(4,128)S(1)}, s32[4,64]{1,0:T(4,128)}, u32[]{:S(2)}) copy-start(s32[4,64]{1,0:T(4,128)} %param.19) | copy-start | bytes 3076
  36.3 31.2 %copy-start.6 = (f32[4,32]{1,0:T(4,128)}, f32[4,32]{1,0:T(4,128)S(1)}, u32[]{:S(2)}) copy-start(f32[4,32]{1,0:T(4,128)S(1)} %fusion.20) | copy-start | bytes 1540
where the time goes:
time: 67.8 us; the launch traced here: 67.5 us
  blocking collectives  57.9 us (85%)
  matrix products  7.18 us (11%)
  between operations  1.57 us (2%)
  local copies, waits for them, and re-layouts  0.91 us (1%)
    psum x1, blocking collectives, body(): picked = lax.psum(picked_local, ('rows', 'seq'))  30.9 us
    psum x1, blocking collectives, body(): total = lax.psum(local, 'seq')  21.5 us
    all_gather x1, blocking collectives, body(): lax.all_gather(test, 'rows', axis=0, tiled=True)  5.43 us
    dot_general x1, matrix products, body(): jnp.einsum('lbto,lbti->lboi', pg, pa, preferred_element_type=jnp.float32)  2.65 us
    dot_general x1, matrix products, body(): jnp.einsum('lbtd,ldr->lbtr', out_grads, proj_out, preferred_element_type=...  2.06 us

commit v1 on v0

--- a/solution.py
+++ b/solution.py
@@ -45,7 +45,7 @@
         jnp.float32
     )
     picked_local = jnp.einsum("bkr,rb->bk", onehot, scores, precision=high)
-    picked = lax.psum(picked_local, ("rows", "seq"))
+    picked = lax.psum(lax.psum(picked_local, "seq"), "rows")
     return (scores, picked)
 
 

time: 67.8 us -> 51.5 us (0.76)
  blocking collectives: 57.9 us -> 41.5 us
    psum x1 -> x2, blocking collectives: 30.9 us -> 14.6 us  [body(): picked = lax.psum(lax.psum(picked_local, 'seq'), 'rows')]
where the time goes in v1:
time: 51.5 us; the launch traced here: 51.2 us
  blocking collectives  41.5 us (81%)
  matrix products  7.18 us (14%)
  between operations  1.57 us (3%)
  local copies, waits for them, and re-layouts  0.91 us (2%)
    psum x1, blocking collectives, body(): total = lax.psum(local, 'seq')  21.5 us
    psum x2, blocking collectives, body(): picked = lax.psum(lax.psum(picked_local, 'seq'), 'rows')  14.6 us
    all_gather x1, blocking collectives, body(): lax.all_gather(test, 'rows', axis=0, tiled=True)  5.43 us
    dot_general x1, matrix products, body(): jnp.einsum('lbto,lbti->lboi', pg, pa, preferred_element_type=jnp.float32)  2.65 us
    dot_general x1, matrix products, body(): jnp.einsum('lbtd,ldr->lbtr', out_grads, proj_out, preferred_element_type=...  2.06 us
    dot_general x1, matrix products, body(): jnp.dot(store, lax.all_gather(test, 'rows', axis=0, tiled=True).T, prefer...  1.29 us

profile of v1, /device:TPU:0, one launch (start us, length us, event | category | flops | bytes accessed | tf_op | source)
XLA Modules:
  0.0 51.2 jit_solution(15397679134452369405)
XLA Ops:
  0.6 0.0 copy-start
  0.6 0.0 copy-start.1
  1.5 0.8 %copy-done = bf16[2,1,128,4096]{3,2,1,0:T(8,128)(2,1)S(1)} copy-done((bf16[2,1,128,4096]{3,2,1,0:T(8,128)(2,1)S(1)}, bf16[2,1,128,4096]{3,2,1,0:T(8,128)(2,1)}, u32[]{:S(2)}) %copy-start) | copy-done | bytes 2097176
  2.2 2.1 %fusion.16 = bf16[2,128,64]{1,2,0:T(8,128)(2,1)S(1)} fusion(bf16[2,4096,64]{1,2,0:T(8,128)(2,1)} %param.14, bf16[2,1,128,4096]{3,2,1,0:T(8,128)(2,1)S(1)} %copy-done, bf16[128]{0:T(256)(128)(2,1)S(1)} %compare_convert_fusion), kind=kOutput, calls=%fused_computation.10 | convolution fusion | flops 134250496 | bytes 3178752 | tf_op jit(solution)/shard_map/lbtd,ldr->lbtr/dot_general | solution.py:27
  4.3 0.0 copy-done.1
  4.3 0.0 copy-start.2
  4.3 0.0 copy-start.3
  4.3 0.0 copy-start.4
  4.4 0.0 copy-start.5
  4.4 2.7 %fusion.14 = f32[2,64,64]{2,1,0:T(8,128)S(1)} fusion(bf16[2,128,64]{1,2,0:T(8,128)(2,1)S(1)} %fusion.16, bf16[2,4096,64]{1,2,0:T(8,128)(2,1)S(1)} %copy-done.1, bf16[2,1,128,4096]{3,2,1,0:T(8,128)(2,1)} %param.10, bf16[128]{0:T(256)(128)(2,1)S(1)} %compare_convert_fusion), kind=kOutput, calls=%fused_computation.9 | convolution fusion | flops 136347648 | bytes 3211520 | tf_op jit(solution)/shard_map/lbto,lbti->lboi/dot_general | solution.py:30
  7.0 21.5 %psum.21 = f32[2,64,64]{2,1,0:T(8,128)S(1)} all-reduce(f32[2,64,64]{2,1,0:T(8,128)S(1)} %fusion.14), channel_id=1, replica_groups=mesh['groups'=2,'rows'=4,'seq'=4] {'seq'}, use_global_device_ids=true, to_apply=%region_0.0 | all-reduce | flops 8192 | bytes 65536 | tf_op jit(solution)/shard_map/psum | solution.py:31
  28.6 0.0 copy-done.2
  28.6 0.3 fusion.25
  28.9 0.0 copy-done.3
  28.9 0.2 convolution_divide_fusion
  29.1 0.2 fusion.26
  29.3 0.2 convolution_convert_fusion
  29.5 0.1 reshape.69
  29.6 5.4 %all-gather = bf16[4,1,8192]{2,1,0:T(2,128)(2,1)S(1)} all-gather(bf16[1,1,8192]{2,1,0:T(2,128)(2,1)S(1)} %reshape.69), channel_id=1, replica_groups=mesh['groups'=2,'rows'=4,'seq'=4] {'rows'}, dimensions={0}, use_global_device_ids=true | all-gather | bytes 81920 | tf_op jit(solution)/shard_map/all_gather | solution.py:38
  35.0 1.3 %fusion.20 = f32[4,32]{1,0:T(4,128)S(1)} fusion(bf16[32,8192]{1,0:T(8,128)(2,1)} %param.18, bf16[4,1,8192]{2,1,0:T(2,128)(2,1)S(1)} %all-gather), kind=kOutput, calls=%fused_computation.13 | convolution fusion | flops 2097152 | bytes 590336 | tf_op jit(solution)/shard_map/dot_general | solution.py:36
  36.3 0.3 fusion.19
  36.6 8.4 %psum.22 = f32[4,64]{1,0:T(4,128)S(1)} all-reduce(f32[4,64]{1,0:T(4,128)S(1)} %bitcast.41), channel_id=1, replica_groups=mesh['groups'=2,'rows'=4,'seq'=4] {'seq'}, use_global_device_ids=true, to_apply=%region_1.0 | all-reduce | flops 256 | bytes 2048 | tf_op jit(solution)/shard_map/psum | solution.py:48
  45.0 6.2 %psum.23 = f32[4,64]{1,0:T(4,128)} all-reduce(f32[4,64]{1,0:T(4,128)S(1)} %psum.22), channel_id=1, replica_groups=mesh['groups'=2,'rows'=4,'seq'=4] {'rows'}, use_global_device_ids=true, to_apply=%region_2.0 | all-reduce | flops 256 | bytes 2048 | tf_op jit(solution)/shard_map/psum | solution.py:48
  51.2 0.0 copy-done.6
  (5 shorter events, 0.0 us)
Async XLA Ops:
  0.6 1.6 %copy-start = (bf16[2,1,128,4096]{3,2,1,0:T(8,128)(2,1)S(1)}, bf16[2,1,128,4096]{3,2,1,0:T(8,128)(2,1)}, u32[]{:S(2)}) copy-start(bf16[2,1,128,4096]{3,2,1,0:T(8,128)(2,1)} %param.11) | copy-start | bytes 6291460
  0.6 3.7 %copy-start.1 = (bf16[2,4096,64]{1,2,0:T(8,128)(2,1)S(1)}, bf16[2,4096,64]{1,2,0:T(8,128)(2,1)}, u32[]{:S(2)}) copy-start(bf16[2,4096,64]{1,2,0:T(8,128)(2,1)} %param.13) | copy-start | bytes 3145732
  4.3 24.2 %copy-start.2 = (f32[2,64,64]{2,1,0:T(8,128)S(1)}, f32[2,64,64]{2,1,0:T(8,128)}, u32[]{:S(2)}) copy-start(f32[2,64,64]{2,1,0:T(8,128)} %param.16) | copy-start | bytes 98308
  4.3 24.5 %copy-start.3 = (f32[2,64,64]{2,1,0:T(8,128)S(1)}, f32[2,64,64]{2,1,0:T(8,128)}, u32[]{:S(2)}) copy-start(f32[2,64,64]{2,1,0:T(8,128)} %param.15) | copy-start | bytes 98308
  4.3 24.5 %copy-start.4 = (f32[2,64,64]{2,1,0:T(8,128)S(1)}, f32[2,64,64]{2,1,0:T(8,128)}, u32[]{:S(2)}) copy-start(f32[2,64,64]{2,1,0:T(8,128)} %param.17) | copy-start | bytes 98308
  4.4 32.0 %copy-start.5 = (s32[4,64]{1,0:T(4,128)S(1)}, s32[4,64]{1,0:T(4,128)}, u32[]{:S(2)}) copy-start(s32[4,64]{1,0:T(4,128)} %param.19) | copy-start | bytes 3076
  36.3 14.9 %copy-start.6 = (f32[4,32]{1,0:T(4,128)}, f32[4,32]{1,0:T(4,128)S(1)}, u32[]{:S(2)}) copy-start(f32[4,32]{1,0:T(4,128)S(1)} %fusion.20) | copy-start | bytes 1540
